TPU v7x, 32 devices: a whole 2x2x4 slice. The times are simulated.
32 devices in a mesh: dp: 8 (over z, y), tensor: 4 (over x, core).
Axes of the slice: x: 2, y: 2, z: 4, core: 2. Of those that a mesh axis runs over, the one named last changes fastest.
Arguments:
- signal: bfloat16 [26112, 512], P('dp', 'tensor'), may hold values from -6 to 6
- horizon: int32 [32], P('dp'), may hold values from 96 to 720, as said below
- down_a: bfloat16 [6144, 512], P('dp', 'tensor'), may hold values from -0.078125 to 0.078125
- iso_a: bfloat16 [34816, 512], P('dp', 'tensor'), may hold values from -0.046875 to 0.046875
- up_a: bfloat16 [512, 12, 512], P('dp', None, 'tensor'), may hold values from -0.25 to 0.25
- down_b: bfloat16 [8192, 512], P('dp', 'tensor'), may hold values from -0.0625 to 0.0625
- iso_b: bfloat16 [26112, 512], P('dp', 'tensor'), may hold values from -0.0546875 to 0.0546875
- up_b: bfloat16 [512, 16, 512], P('dp', None, 'tensor'), may hold values from -0.25 to 0.25
- merge_w: bfloat16 [1024, 512], P('dp', 'tensor'), may hold values from -0.1875 to 0.1875
- ff_in: bfloat16 [512, 2048], P(None, 'tensor'), may hold values from -0.25 to 0.25
- ff_out: bfloat16 [2048, 512], P('tensor'), may hold values from -0.125 to 0.125
- norm_gain: float32 [512], P('tensor'), may hold values from 0.1 to 1.9
- norm_bias: float32 [512], P('tensor'), may hold values from -4 to 4
- first_gain: float32 [512], P('tensor'), may hold values from 0.1 to 1.9
- first_bias: float32 [512], P('tensor'), may hold values from -4 to 4
- last_gain: float32 [512], P('tensor'), may hold values from 0.1 to 1.9
- last_bias: float32 [512], P('tensor'), may hold values from -4 to 4
- cotangent: bfloat16 [26112, 512], P('dp', 'tensor'), may hold values from -6 to 6
Outputs:
- series_out: bfloat16 [26112, 512], P('dp', 'tensor')
- grad_input: float32 [26112, 512], P('dp', 'tensor')
- grad_down_a: float32 [6144, 512], P('dp', 'tensor')
- grad_iso_a: float32 [34816, 512], P('dp', 'tensor')
- grad_up_a: float32 [512, 12, 512], P('dp', None, 'tensor')
- grad_down_b: float32 [8192, 512], P('dp', 'tensor')
- grad_iso_b: float32 [26112, 512], P('dp', 'tensor')
- grad_up_b: float32 [512, 16, 512], P('dp', None, 'tensor')
- grad_merge: float32 [1024, 512], P('dp', 'tensor')
- grad_ff_in: float32 [512, 2048], P(None, 'tensor')
- grad_ff_out: float32 [2048, 512], P('tensor')
- grad_norm_gain: float32 [512], P('tensor')
- grad_norm_bias: float32 [512], P('tensor')
- grad_first_gain: float32 [512], P('tensor')
- grad_first_bias: float32 [512], P('tensor')
- grad_last_gain: float32 [512], P('tensor')
- grad_last_bias: float32 [512], P('tensor')
Inputs may be any that keep to these rules, and one draw needn't show every extreme that they name: Each series' horizon is one of 96, 192, 336 and 720; some series has 720.
All inputs are finite; a program needn't handle non-finite values.
Results may differ from a plain program's by a relative error of at most 0.014.
Values may be sent and summed in bfloat16 or wider, within the bound.
No kernel may reach another device: no remote copies, remote signals or barrier semaphores. Data moves between devices by JAX's collectives and lax.ppermute only.
A program may use at most 384 MiB of HBM per device.

v0:
```python
from functools import partial
import jax
import jax.numpy as jnp
from jax import lax
from jax.sharding import PartitionSpec as P

D = 512
SA = 12
SB = 16
IN_LEN = 96
L = 816
MA = 68
MB = 51
EPS = 1e-05
BF = jnp.bfloat16
F32 = jnp.float32


def matmul(left, right):
    return jnp.dot(left, right, preferred_element_type=F32)


def over_rows(left, right):
    return lax.dot_general(left, right, (((0,), (0,)), ((), ())), preferred_element_type=F32)


def against(left, right):
    return lax.dot_general(left, right, (((1,), (1,)), ((), ())), preferred_element_type=F32)


def swap(value, mask):
    return lax.ppermute(value, "tensor", [(i, i ^ mask) for i in range(4)])


def by_xor(blocks):
    t = lax.axis_index("tensor")
    low = t % 2 == 0
    high = t // 2 == 0
    mid = [jnp.where(low, blocks[k], blocks[k ^ 1]) for k in range(4)]
    return [jnp.where(high, mid[k], mid[k ^ 2]) for k in range(4)]


def lanes(value):
    width = value.shape[1] // 4
    return [value[:, i * width : (i + 1) * width] for i in range(4)]


def own_lanes(value):
    width = value.shape[1] // 4
    return lax.dynamic_slice_in_dim(value, lax.axis_index("tensor") * width, width, 1)


def gather_blocks(value):
    across = swap(value, 2)
    return by_xor([value, swap(value, 1), across, swap(across, 1)])


def channel_gather(value):
    return jnp.concatenate(gather_blocks(value), axis=1)


def to_rows(value):
    t = lax.axis_index("tensor")
    count = value.shape[0] // 4
    send = [lax.dynamic_slice_in_dim(value, (t ^ k) * count, count, 0) for k in range(4)]
    return jnp.concatenate(by_xor([send[0]] + [swap(send[k], k) for k in (1, 2, 3)]), axis=1)


def to_channels(value):
    send = by_xor(lanes(value))
    return jnp.concatenate(by_xor([send[0]] + [swap(send[k], k) for k in (1, 2, 3)]), axis=0)


def quarter_sum(blocks):
    send = by_xor(blocks)
    mine = send[0] + swap(send[1].astype(BF), 1).astype(F32)
    other = send[2] + swap(send[3].astype(BF), 1).astype(F32)
    return mine + swap(other.astype(BF), 2).astype(F32)


def ring_order(count):
    return list(range(0, count, 2)) + list(range(1, count, 2))[::-1]


def ring_gather(value):
    count = lax.axis_size("dp")
    order = ring_order(count)
    table = jnp.array(order, jnp.int32)
    place = jnp.array([order.index(i) for i in range(count)], jnp.int32)[lax.axis_index("dp")]
    up = [(order[i], order[(i + 1) % count]) for i in range(count)]
    down = [(b, a) for a, b in up]
    result = jnp.zeros((count,) + value.shape, value.dtype)
    result = lax.dynamic_update_index_in_dim(result, value, lax.axis_index("dp"), 0)
    ahead = behind = value
    for step in range(1, count // 2 + 1):
        ahead = lax.ppermute(ahead, "dp", up)
        result = lax.dynamic_update_index_in_dim(result, ahead, table[(place - step) % count], 0)
        if step <= (count - 1) // 2:
            behind = lax.ppermute(behind, "dp", down)
            result = lax.dynamic_update_index_in_dim(
                result, behind, table[(place + step) % count], 0
            )
    return result


def exchange_sum(blocks):
    got = lax.all_to_all(blocks.astype(BF), "dp", 0, 0, tiled=True)
    return jnp.sum(got.astype(F32), axis=0)


def scatter_sum(value):
    return lax.psum_scatter(value.astype(BF), "dp", scatter_dimension=0, tiled=True).astype(F32)


def norm_forward(operand, gain_vec, bias_vec):
    row_mean = jnp.mean(operand, axis=1, keepdims=True)
    row_square = jnp.mean(operand * operand, axis=1, keepdims=True)
    inv_std = lax.rsqrt(row_square - row_mean * row_mean + EPS)
    normed = (operand - row_mean) * inv_std
    return (normed * gain_vec + bias_vec, (normed, inv_std))


def norm_backward(upstream, gain_vec, stored):
    normed, inv_std = stored
    scaled = upstream * gain_vec
    first_mean = jnp.mean(scaled, axis=1, keepdims=True)
    second_mean = jnp.mean(scaled * normed, axis=1, keepdims=True)
    result = inv_std * (scaled - first_mean - normed * second_mean)
    return (result, jnp.sum(upstream * normed, axis=0), jnp.sum(upstream, axis=0))


def tap_plan(rows_held):
    count = lax.axis_size("dp")
    taps = max((-(-(i * rows_held % D + rows_held) // D) for i in range(count)))
    start = lax.axis_index("dp") * rows_held
    return (taps, start // D, start % D)


def iso_forward(act_all, weight, span_len):
    groups = act_all.shape[0]
    series = act_all.shape[1] // span_len
    taps, first, offset = tap_plan(weight.shape[0])
    wide = lax.dynamic_update_slice_in_dim(
        jnp.zeros((taps * D, weight.shape[1]), BF), weight, offset, 0
    )
    timed = act_all.reshape(groups, series, span_len, D).transpose(2, 0, 1, 3)
    timed = timed.reshape(span_len, groups * series, D)
    timed = jnp.pad(timed, ((span_len - 1, taps), (0, 0), (0, 0)))
    timed = lax.dynamic_slice_in_dim(timed, first, span_len + taps - 1, 0)
    columns = jnp.concatenate([timed[j : j + span_len] for j in range(taps)], axis=2)
    columns = columns.reshape(span_len * groups * series, taps * D)
    pre = matmul(columns, wide).reshape(span_len, groups, series, -1)
    pre = pre.transpose(1, 2, 0, 3).reshape(groups, series * span_len, -1)
    return (pre, (columns, wide))


def iso_backward(grad_all, stored, rows_held, span_len):
    columns, wide = stored
    groups = grad_all.shape[0]
    series = grad_all.shape[1] // span_len
    taps, first, offset = tap_plan(rows_held)
    timed = grad_all.reshape(groups, series, span_len, -1).transpose(2, 0, 1, 3)
    timed = timed.reshape(span_len * groups * series, -1)
    grad_wide = over_rows(columns, timed)
    grad_weight = lax.dynamic_slice_in_dim(grad_wide, offset, rows_held, 0)
    spread = against(timed, wide).reshape(span_len, groups * series, taps * D)
    total = jnp.zeros((span_len + taps - 1, groups * series, D), F32)
    for j in range(taps):
        total = total.at[j : j + span_len].add(spread[:, :, j * D : (j + 1) * D])
    padded = jnp.zeros((2 * span_len - 1 + taps, groups * series, D), F32)
    padded = lax.dynamic_update_slice_in_dim(padded, total, first, 0)
    back = padded[span_len - 1 : 2 * span_len - 1].reshape(span_len, groups, series, D)
    return (grad_weight, back.transpose(1, 2, 0, 3).reshape(groups, series * span_len, D))


def body(
    signal,
    horizon,
    down_a,
    iso_a,
    up_a,
    down_b,
    iso_b,
    up_b,
    merge_w,
    ff_in,
    ff_out,
    norm_gain,
    norm_bias,
    first_gain,
    first_bias,
    last_gain,
    last_bias,
    cotangent,
):
    row_count, col_count = signal.shape
    part_rows = row_count // 4
    series_count = row_count // L
    short_a = row_count // SA
    short_b = row_count // SB
    t = lax.axis_index("tensor")
    wd_a = ring_gather(down_a).reshape(SA * D, col_count)
    wd_b = ring_gather(down_b).reshape(SB * D, col_count)
    x_full = channel_gather(signal)
    vectors = channel_gather(
        jnp.stack([norm_gain, norm_bias, first_gain, first_bias, last_gain, last_bias])
    )
    n_gain, n_bias, f_gain, f_bias, l_gain, l_bias = (vectors[i : i + 1] for i in range(6))
    cot_rows = to_rows(cotangent)
    wu_a = lax.all_gather(up_a, "dp", axis=0, tiled=True).reshape(D, SA * col_count)
    wu_b = lax.all_gather(up_b, "dp", axis=0, tiled=True).reshape(D, SB * col_count)
    w_merge = channel_gather(ring_gather(merge_w).reshape(2 * D, col_count))
    w_in = channel_gather(ff_in)
    w_out = jnp.concatenate(gather_blocks(ff_out), axis=0)
    window_a = x_full.reshape(short_a, SA * D)
    window_b = x_full.reshape(short_b, SB * D)
    down_act = jnp.concatenate(
        [jnp.tanh(matmul(window_a, wd_a)), jnp.tanh(matmul(window_b, wd_b))], axis=0
    )
    down_low = down_act.astype(BF)
    high = t // 2 == 0
    low = t % 2 == 0
    across = swap(down_low, 2)
    pair = jnp.concatenate(
        [jnp.where(high, down_low, across), jnp.where(high, across, down_low)], axis=1
    )
    pair_all = ring_gather(pair)
    mate_all = swap(pair_all, 1)
    even = jnp.where(low, pair_all, mate_all)
    odd = jnp.where(low, mate_all, pair_all)
    down_all = jnp.concatenate(
        [even[..., :col_count], odd[..., :col_count], even[..., col_count:], odd[..., col_count:]],
        axis=2,
    )
    down_full = lax.dynamic_index_in_dim(down_all, lax.axis_index("dp"), 0, keepdims=False)
    part_a, iso_store_a = iso_forward(down_all[:, :short_a], iso_a, MA)
    part_b, iso_store_b = iso_forward(down_all[:, short_a:], iso_b, MB)
    iso_pre = exchange_sum(jnp.concatenate([part_a, part_b], axis=1))
    iso_act = jnp.tanh(channel_gather(iso_pre))
    middle, store_mid = norm_forward(iso_act + down_full.astype(F32), n_gain, n_bias)
    middle = middle.astype(BF)
    up_act_a = jnp.tanh(matmul(middle[:short_a], wu_a).reshape(row_count, col_count))
    up_act_b = jnp.tanh(matmul(middle[short_a:], wu_b).reshape(row_count, col_count))
    x_rows = lax.dynamic_slice_in_dim(x_full, t * part_rows, part_rows, 0).astype(F32)
    branch_a, store_br_a = norm_forward(
        to_rows(up_act_a.astype(BF)).astype(F32) + x_rows, n_gain, n_bias
    )
    branch_b, store_br_b = norm_forward(
        to_rows(up_act_b.astype(BF)).astype(F32) + x_rows, n_gain, n_bias
    )
    merge_in = jnp.concatenate([branch_a.astype(BF), branch_b.astype(BF)], axis=1)
    merged = matmul(merge_in, w_merge)
    first_out, store_first = norm_forward(merged, f_gain, f_bias)
    first_low = first_out.astype(BF)
    hidden_pre = matmul(first_low, w_in)
    hidden = jax.nn.gelu(hidden_pre, approximate=False).astype(BF)
    feed = matmul(hidden, w_out)
    last_out, store_last = norm_forward(merged + feed, l_gain, l_bias)
    position = t * part_rows + lax.broadcasted_iota(jnp.int32, (part_rows, 1), 0)
    limit = jnp.broadcast_to(horizon[:, None], (series_count, L)).reshape(row_count, 1)
    limit = lax.dynamic_slice_in_dim(limit, t * part_rows, part_rows, 0)
    out_mask = (position % L < IN_LEN + limit).astype(F32)
    series_out = to_channels((last_out * out_mask).astype(BF))
    upstream = cot_rows.astype(F32) * out_mask
    grad_sum, grad_last_gain, grad_last_bias = norm_backward(upstream, l_gain, store_last)
    grad_feed = grad_sum.astype(BF)
    grad_ff_out = over_rows(hidden, grad_feed)
    grad_hidden = against(grad_feed, w_out)
    _, gelu_back = jax.vjp(partial(jax.nn.gelu, approximate=False), hidden_pre)
    grad_hpre = gelu_back(grad_hidden)[0].astype(BF)
    grad_ff_in = over_rows(first_low, grad_hpre)
    grad_first = against(grad_hpre, w_in)
    grad_merged_norm, grad_first_gain, grad_first_bias = norm_backward(
        grad_first, f_gain, store_first
    )
    grad_merged = (grad_merged_norm + grad_sum).astype(BF)
    grad_merge = over_rows(merge_in, grad_merged)
    grad_pair = against(grad_merged, w_merge)
    grad_resid_a, gain_one, bias_one = norm_backward(grad_pair[:, :D], n_gain, store_br_a)
    grad_resid_b, gain_two, bias_two = norm_backward(grad_pair[:, D:], n_gain, store_br_b)
    resid_a = to_channels(grad_resid_a.astype(BF)).astype(F32)
    resid_b = to_channels(grad_resid_b.astype(BF)).astype(F32)
    grad_upre_a = (resid_a * (1.0 - up_act_a * up_act_a)).astype(BF).reshape(short_a, -1)
    grad_upre_b = (resid_b * (1.0 - up_act_b * up_act_b)).astype(BF).reshape(short_b, -1)
    part_mid = jnp.concatenate([against(grad_upre_a, wu_a), against(grad_upre_b, wu_b)], axis=0)
    grad_up_a = over_rows(middle[:short_a], grad_upre_a).reshape(D, SA, col_count)
    grad_up_b = over_rows(middle[short_a:], grad_upre_b).reshape(D, SB, col_count)
    blocks = lanes(part_mid)
    keep = jnp.concatenate(
        [jnp.where(low, blocks[0], blocks[1]), jnp.where(low, blocks[2], blocks[3])], axis=1
    )
    give = jnp.concatenate(
        [jnp.where(low, blocks[1], blocks[0]), jnp.where(low, blocks[3], blocks[2])], axis=1
    )
    keep = keep + swap(give, 1)
    keep = keep + swap(keep, 2)
    mate = swap(keep, 1)
    even = jnp.where(low, keep, mate)
    odd = jnp.where(low, mate, keep)
    grad_middle = jnp.concatenate(
        [even[:, :col_count], odd[:, :col_count], even[:, col_count:], odd[:, col_count:]], axis=1
    )
    grad_inner, gain_mid, bias_mid = norm_backward(grad_middle, n_gain, store_mid)
    grad_ipre = own_lanes((grad_inner * (1.0 - iso_act * iso_act)).astype(BF))
    grad_ipre_all = ring_gather(grad_ipre)
    grad_iso_a, back_a = iso_backward(grad_ipre_all[:, :short_a], iso_store_a, iso_a.shape[0], MA)
    grad_iso_b, back_b = iso_backward(grad_ipre_all[:, short_a:], iso_store_b, iso_b.shape[0], MB)
    back = jnp.concatenate([back_a, back_b], axis=1)
    groups = back.shape[0]
    back = quarter_sum([back[..., i * col_count : (i + 1) * col_count] for i in range(4)])
    grad_down = exchange_sum(back)
    grad_dpre = ((grad_down + own_lanes(grad_inner)) * (1.0 - down_act * down_act)).astype(BF)
    grad_dpre_a, grad_dpre_b = (grad_dpre[:short_a], grad_dpre[short_a:])
    grad_down_a = over_rows(window_a, grad_dpre_a)
    grad_down_b = over_rows(window_b, grad_dpre_b)
    grad_x = against(grad_dpre_a, wd_a).reshape(row_count, D) + against(grad_dpre_b, wd_b).reshape(
        row_count, D
    )
    grad_input = quarter_sum(lanes(grad_x)) + resid_a + resid_b
    sum_up_a = scatter_sum(grad_up_a)
    sum_up_b = scatter_sum(grad_up_b)
    sum_down_a = scatter_sum(grad_down_a)
    sum_down_b = scatter_sum(grad_down_b)
    sum_merge = scatter_sum(quarter_sum(lanes(grad_merge)))
    ff_own = jnp.concatenate(
        [
            quarter_sum(lanes(grad_ff_in)),
            quarter_sum([grad_ff_out[i * D : (i + 1) * D] for i in range(4)]),
        ],
        axis=0,
    )
    ff_total = ring_gather(scatter_sum(ff_own).astype(BF)).reshape(2 * D, D).astype(F32)
    sums = jnp.stack(
        [
            gain_one + gain_two + 0.25 * gain_mid,
            bias_one + bias_two + 0.25 * bias_mid,
            grad_first_gain,
            grad_first_bias,
            grad_last_gain,
            grad_last_bias,
        ]
    )
    sums = own_lanes(lax.psum(sums, ("dp", "tensor")))
    return (
        series_out,
        grad_input,
        sum_down_a,
        grad_iso_a,
        sum_up_a,
        sum_down_b,
        grad_iso_b,
        sum_up_b,
        sum_merge,
        ff_total[:D],
        ff_total[D:],
        sums[0],
        sums[1],
        sums[2],
        sums[3],
        sums[4],
        sums[5],
    )


def solution(mesh):
    in_specs = (
        P("dp", "tensor"),
        P("dp"),
        P("dp", "tensor"),
        P("dp", "tensor"),
        P("dp", None, "tensor"),
        P("dp", "tensor"),
        P("dp", "tensor"),
        P("dp", None, "tensor"),
        P("dp", "tensor"),
        P(None, "tensor"),
        P("tensor", None),
        P("tensor"),
        P("tensor"),
        P("tensor"),
        P("tensor"),
        P("tensor"),
        P("tensor"),
        P("dp", "tensor"),
    )
    out_specs = (
        P("dp", "tensor"),
        P("dp", "tensor"),
        P("dp", "tensor"),
        P("dp", "tensor"),
        P("dp", None, "tensor"),
        P("dp", "tensor"),
        P("dp", "tensor"),
        P("dp", None, "tensor"),
        P("dp", "tensor"),
        P(None, "tensor"),
        P("tensor", None),
        P("tensor"),
        P("tensor"),
        P("tensor"),
        P("tensor"),
        P("tensor"),
        P("tensor"),
    )
    return jax.shard_map(body, mesh=mesh, in_specs=in_specs, out_specs=out_specs, check_vma=False)
```

profile of v0, /device:TPU:0, one launch (start us, length us, event | category | flops | bytes accessed | tf_op | source)
XLA Modules:
  0.0 962.9 jit_solution(12522362180640404888)
XLA Ops:
  41.1 11.8 %collective-permute-done.11 = bf16[1024,128]{1,0:T(8,128)(2,1)S(1)} collective-permute-done((bf16[1024,128]{1,0:T(8,128)(2,1)S(1)}, bf16[1024,128]{1,0:T(8,128)(2,1)S(1)}, u32[]{:S(2)}, u32[]{:S(2)}) %collective-permute-start.11) | collective-permute-done | bytes 262176 | tf_op jit(solution)/shard_map/ppermute | solution.py:99
  55.0 6.5 collective-permute-done.6
  80.7 4.2 collective-permute-done.16
  87.6 5.0 reshape.927
  101.8 4.3 collective-permute-done.17
  120.4 10.6 %collective-permute-done.21 = bf16[476,256]{1,0:T(8,128)(2,1)S(1)} collective-permute-done((bf16[476,256]{1,0:T(8,128)(2,1)S(1)}, bf16[476,256]{1,0:T(8,128)(2,1)S(1)}, u32[]{:S(2)}, u32[]{:S(2)}) %collective-permute-start.21) | collective-permute-done | bytes 243744 | tf_op jit(solution)/shard_map/ppermute | solution.py:99
  133.2 5.9 collective-permute-done.23
  172.6 21.0 %fusion.53 = bf16[8,4,68,128]{3,2,1,0:T(8,128)(2,1)S(1)} fusion(bf16[68,8,4,4608]{3,0,2,1:T(8,128)(2,1)S(1)} %bitcast.258, bf16[4608,128]{1,0:T(8,128)(2,1)} %constant_dynamic-update-slice_fusion), kind=kOutput, calls=%fused_computation.173 | convolution fusion | flops 2567192576 | bytes 21790720 | tf_op jit(solution)/shard_map/dot_general | solution.py:20
  212.4 22.6 %dot_general.101 = bf16[51,8,4,4096]{3,2,1,0:T(4,128)(2,1)} reshape(bf16[51,32,4096]{2,1,0:T(8,128)(2,1)} %fusion.38) | data formatting | bytes 26738688 | tf_op jit(solution)/shard_map/dot_general | solution.py:20
  235.0 10.3 %fusion.54 = bf16[8,4,51,128]{3,1,0,2:T(4,128)(2,1)S(1)} fusion(bf16[51,8,4,4096]{3,2,1,0:T(4,128)(2,1)} %dot_general.101, bf16[4096,128]{1,0:T(8,128)(2,1)} %constant_dynamic-update-slice_fusion.2), kind=kOutput, calls=%fused_computation.174 | convolution fusion | flops 1711484928 | bytes 14835712 | tf_op jit(solution)/shard_map/dot_general | solution.py:20
  246.6 4.5 all-to-all-start
  253.2 13.6 %collective-permute-done.42 = bf16[128,128]{1,0:T(8,128)(2,1)S(1)} collective-permute-done((bf16[128,128]{1,0:T(8,128)(2,1)S(1)}, bf16[128,128]{1,0:T(8,128)(2,1)S(1)}, u32[]{:S(2)}, u32[]{:S(2)}) %collective-permute-start.42) | collective-permute-done | bytes 32800 | tf_op jit(solution)/shard_map/ppermute | solution.py:96
  266.9 8.5 collective-permute-done.43
  284.2 4.9 collective-permute-done.58
  289.1 5.6 collective-permute-done.46
  350.4 19.4 %multiply_convert_fusion = (bf16[816,2048]{1,0:T(8,128)(2,1)S(1)}, f32[816,2048]{1,0:T(8,128)}, f32[816,2048]{1,0:T(8,128)}) fusion(bf16[512,512]{1,0:T(8,128)(2,1)S(1)} %copy-done.71, bf16[512,512]{1,0:T(8,128)(2,1)S(1)} %copy-done.70, bf16[512,512]{1,0:T(8,128)(2,1)S(1)} %copy-done.69, bf16[512,512]{1,0:T(8,128)(2,1)S(1)} %copy-done.68, ...), kind=kOutput, calls=%fused_computation.28 | convolution fusion | flops 1830379520 | bytes 20490624 | tf_op jit(solution)/shard_map/dot_general | solution.py:20
  373.6 7.2 add_convert_fusion
  445.6 18.4 %collective-permute-done.67 = f32[476,256]{1,0:T(8,128)} collective-permute-done((f32[476,256]{1,0:T(8,128)}, f32[476,256]{1,0:T(8,128)}, u32[]{:S(2)}, u32[]{:S(2)}) %collective-permute-start.67) | collective-permute-done | bytes 487456 | tf_op jit(solution)/shard_map/ppermute | solution.py:32
  468.7 5.5 collective-permute-done.90
  491.9 21.0 %copy.121 = bf16[68,32,4608]{2,1,0:T(8,128)(2,1)} copy(bf16[68,32,4608]{2,0,1:T(8,128)(2,1)} %copy-done.11) | data formatting | bytes 40108032 | tf_op jit(solution)/shard_map/concatenate | solution.py:150
  518.0 6.4 dynamic_update_slice.196
  524.8 6.4 dynamic_update_slice.197
  531.2 6.4 dynamic_update_slice.198
  538.0 6.4 dynamic_update_slice.199
  544.4 6.4 dynamic_update_slice.200
  551.3 6.4 dynamic_update_slice.201
  557.7 6.4 dynamic_update_slice.202
  564.3 6.4 dynamic_update_slice.203
  571.1 17.3 %fusion.56 = f32[68,32,4608]{2,1,0:T(8,128)} fusion(bf16[68,32,128]{2,1,0:T(8,128)(2,1)S(1)} %bitcast.272, bf16[4608,128]{1,0:T(8,128)(2,1)} %constant_dynamic-update-slice_fusion), kind=kOutput, calls=%fused_computation.176 | convolution fusion | flops 2566914048 | bytes 41844736 | tf_op jit(solution)/shard_map/dot_general | solution.py:28
  619.4 5.5 copy.116
  624.9 4.9 broadcast_in_dim.247
  629.8 22.3 %dynamic_update_slice.204 = f32[144,32,512]{2,0,1:T(8,128)} dynamic-update-slice(f32[144,32,512]{2,0,1:T(8,128)} %broadcast_in_dim.247, f32[76,32,512]{2,0,1:T(8,128)} %copy.116, s32[]{:T(128)S(6)} %select_n.1414, s32[]{:T(128)} %constant.1016.clone.1, s32[]{:T(128)} %constant.1016.clone.1) | dynamic-update-slice | bytes 9961476 | tf_op jit(solution)/shard_map/dynamic_update_slice | solution.py:171
  655.2 4.6 copy.117
  659.9 12.2 %fusion.61 = f32[51,32,4096]{2,1,0:T(8,128)} fusion(bf16[51,32,128]{2,1,0:T(8,128)(2,1)S(1)} %bitcast.274, bf16[4096,128]{1,0:T(8,128)(2,1)} %constant_dynamic-update-slice_fusion.2), kind=kOutput, calls=%fused_computation.185 | convolution fusion | flops 1711276032 | bytes 28205056 | tf_op jit(solution)/shard_map/dot_general | solution.py:28
  725.6 53.8 %psum.7 = f32[6,512]{1,0:T(8,128)S(1)} all-reduce(f32[6,512]{1,0:T(8,128)S(1)} %stack.49), channel_id=1, replica_groups=mesh['dp'=8,'tensor'=4] {'dp','tensor'}, use_global_device_ids=true, to_apply=%region_38.39 | all-reduce | flops 3072 | bytes 24576 | tf_op jit(solution)/shard_map/psum | solution.py:343
  783.5 4.9 all-to-all-start.1
  788.4 7.0 fusion.119
  796.8 16.2 %all-to-all-done.1 = bf16[8,476,128]{2,1,0:T(8,128)(2,1)} async-done(((bf16[8,476,128]{2,1,0:T(8,128)(2,1)}), bf16[8,476,128]{2,1,0:T(8,128)(2,1)}, u32[]{:S(2)}, u32[]{:S(2)}) %all-to-all-start.1) | async-done | bytes 974880 | tf_op jit(solution)/shard_map/all_to_all | solution.py:107
  818.8 10.2 %fusion.118 = f32[4608,128]{1,0:T(8,128)S(1)} fusion(bf16[2176,4608]{1,0:T(8,128)(2,1)} %bitcast.259, bf16[2176,128]{1,0:T(8,128)(2,1)} %bitcast.273), kind=kOutput, calls=%fused_computation.513 | convolution fusion | flops 2566914048 | bytes 22970368 | tf_op jit(solution)/shard_map/dot_general | solution.py:24
  844.1 8.4 reshape.948
  856.2 7.9 reshape.947
  864.2 9.4 add.1215
  876.3 4.3 select_convert_fusion.3
  886.3 4.1 collective-permute-done.95
  890.4 4.3 add_convert_fusion.3
  899.9 16.2 %collective-permute-done.81 = bf16[3264,128]{1,0:T(8,128)(2,1)} collective-permute-done((bf16[3264,128]{1,0:T(8,128)(2,1)}, bf16[3264,128]{1,0:T(8,128)(2,1)}, u32[]{:S(2)}, u32[]{:S(2)}) %collective-permute-start.81) | collective-permute-done | bytes 835616 | tf_op jit(solution)/shard_map/ppermute | solution.py:32
  916.2 8.2 add_add_fusion
  926.1 27.7 %reduce-scatter.11.cloned.1.call-done = bf16[1024,128]{1,0:T(8,128)(2,1)} async-done(((bf16[8192,128]{1,0:T(8,128)(2,1)}), bf16[1024,128]{1,0:T(8,128)(2,1)}) %reduce-scatter.11.cloned.1.call-update) | async-done | bytes 262160 | tf_op jit(solution)/shard_map/reduce_scatter | solution.py:112
  (662 shorter events, 416.0 us)
Async XLA Ops:
  7.2 306.6 %all-gather.3.cloned.1.call-start = ((), (), s32[]{:S(2)}) async-start(), calls=%async_computation.8 | async-start | bytes 1769472 | tf_op jit(solution)/shard_map/all_gather | solution.py:210
  7.2 29.3 %collective-permute-start.3 = (bf16[768,128]{1,0:T(8,128)(2,1)}, bf16[768,128]{1,0:T(8,128)(2,1)}, u32[]{:S(2)}, u32[]{:S(2)}) collective-permute-start(bf16[768,128]{1,0:T(8,128)(2,1)} %param.66), channel_id=1, source_target_pairs={{0,8},{8,16},{16,24},{24,28},{28,20},{20,12},{12,4},{4,0},{1,9},{9... | collective-permute-start | bytes 589832 | tf_op jit(solution)/shard_map/ppermute | solution.py:96
  10.3 27.7 %collective-permute-start.4 = (bf16[768,128]{1,0:T(8,128)(2,1)}, bf16[768,128]{1,0:T(8,128)(2,1)}, u32[]{:S(2)}, u32[]{:S(2)}) collective-permute-start(bf16[768,128]{1,0:T(8,128)(2,1)} %param.66), channel_id=1, source_target_pairs={{8,0},{16,8},{24,16},{28,24},{20,28},{12,20},{4,12},{0,4},{9,1},{1... | collective-permute-start | bytes 589832 | tf_op jit(solution)/shard_map/ppermute | solution.py:99
  10.3 66.1 %collective-permute-start.1 = (bf16[3264,128]{1,0:T(8,128)(2,1)}, bf16[3264,128]{1,0:T(8,128)(2,1)S(1)}, u32[]{:S(2)}, u32[]{:S(2)}) collective-permute-start(bf16[3264,128]{1,0:T(8,128)(2,1)} %param.64), channel_id=1, source_target_pairs={{0,2},{1,3},{2,0},{3,1},{4,6},{5,7},{6,4},{7,5},{8,10},{9,11},{10,... | collective-permute-start | bytes 2506760 | tf_op jit(solution)/shard_map/ppermute | solution.py:32
  12.3 72.7 %collective-permute-start = (bf16[3264,128]{1,0:T(8,128)(2,1)}, bf16[3264,128]{1,0:T(8,128)(2,1)}, u32[]{:S(2)}, u32[]{:S(2)}) collective-permute-start(bf16[3264,128]{1,0:T(8,128)(2,1)} %param.64), channel_id=1, source_target_pairs={{0,1},{1,0},{2,3},{3,2},{4,5},{5,4},{6,7},{7,6},{8,9},{9,8},{10,11... | collective-permute-start | bytes 2506760 | tf_op jit(solution)/shard_map/ppermute | solution.py:32
  12.3 28.3 %collective-permute-start.10 = (bf16[1024,128]{1,0:T(8,128)(2,1)}, bf16[1024,128]{1,0:T(8,128)(2,1)S(1)}, u32[]{:S(2)}, u32[]{:S(2)}) collective-permute-start(bf16[1024,128]{1,0:T(8,128)(2,1)} %param.69), channel_id=1, source_target_pairs={{0,8},{8,16},{16,24},{24,28},{28,20},{20,12},{12,4},{4,0},{1,9},{9... | collective-permute-start | bytes 786440 | tf_op jit(solution)/shard_map/ppermute | solution.py:96
  13.9 305.4 %all-gather.5.cloned.1.call-start = ((), (), s32[]{:S(2)}) async-start(), calls=%async_computation.9 | async-start | bytes 2359296 | tf_op jit(solution)/shard_map/all_gather | solution.py:211
  36.5 16.4 %collective-permute-start.11 = (bf16[1024,128]{1,0:T(8,128)(2,1)S(1)}, bf16[1024,128]{1,0:T(8,128)(2,1)S(1)}, u32[]{:S(2)}, u32[]{:S(2)}) collective-permute-start(bf16[1024,128]{1,0:T(8,128)(2,1)S(1)} %copy-done.76), channel_id=1, source_target_pairs={{8,0},{16,8},{24,16},{28,24},{20,28},{12,20},{4,12},{0,4},{9,1},{1... | collective-permute-start | bytes 786440 | tf_op jit(solution)/shard_map/ppermute | solution.py:99
  38.0 15.2 %collective-permute-start.5 = (bf16[768,128]{1,0:T(8,128)(2,1)}, bf16[768,128]{1,0:T(8,128)(2,1)S(1)}, u32[]{:S(2)}, u32[]{:S(2)}) collective-permute-start(bf16[768,128]{1,0:T(8,128)(2,1)} %collective-permute-done.3), channel_id=1, source_target_pairs={{0,8},{8,16},{16,24},{24,28},{28,20},{20,12},{12,4},{4,0},{1,9},{9... | collective-permute-start | bytes 589832 | tf_op jit(solution)/shard_map/ppermute | solution.py:96
  40.6 20.9 %collective-permute-start.6 = (bf16[768,128]{1,0:T(8,128)(2,1)}, bf16[768,128]{1,0:T(8,128)(2,1)S(1)}, u32[]{:S(2)}, u32[]{:S(2)}) collective-permute-start(bf16[768,128]{1,0:T(8,128)(2,1)} %collective-permute-done.4), channel_id=1, source_target_pairs={{8,0},{16,8},{24,16},{28,24},{20,28},{12,20},{4,12},{0,4},{9,1},{1... | collective-permute-start | bytes 589832 | tf_op jit(solution)/shard_map/ppermute | solution.py:99
  53.2 14.9 %collective-permute-start.13 = (bf16[1024,128]{1,0:T(8,128)(2,1)S(1)}, bf16[1024,128]{1,0:T(8,128)(2,1)S(1)}, u32[]{:S(2)}, u32[]{:S(2)}) collective-permute-start(bf16[1024,128]{1,0:T(8,128)(2,1)S(1)} %collective-permute-done.11), channel_id=1, source_target_pairs={{8,0},{16,8},{24,16},{28,24},{20,28},{12,20},{4,12},{0,4},{9,1},{1... | collective-permute-start | bytes 786440 | tf_op jit(solution)/shard_map/ppermute | solution.py:99
  106.9 171.4 %collective-permute-start.30 = (f32[6,128]{1,0:T(8,128)S(1)}, f32[6,128]{1,0:T(8,128)S(1)}, u32[]{:S(2)}, u32[]{:S(2)}) collective-permute-start(f32[6,128]{1,0:T(8,128)S(1)} %stack.44), channel_id=1, source_target_pairs={{0,2},{1,3},{2,0},{3,1},{4,6},{5,7},{6,4},{7,5},{8,10},{9,11},{10,... | collective-permute-start | bytes 9224 | tf_op jit(solution)/shard_map/ppermute | solution.py:32
  107.5 173.6 %collective-permute-start.29 = (f32[6,128]{1,0:T(8,128)S(1)}, f32[6,128]{1,0:T(8,128)S(1)}, u32[]{:S(2)}, u32[]{:S(2)}) collective-permute-start(f32[6,128]{1,0:T(8,128)S(1)} %stack.44), channel_id=1, source_target_pairs={{0,1},{1,0},{2,3},{3,2},{4,5},{5,4},{6,7},{7,6},{8,9},{9,8},{10,11... | collective-permute-start | bytes 9224 | tf_op jit(solution)/shard_map/ppermute | solution.py:32
  107.5 40.9 %collective-permute-start.38 = (bf16[128,128]{1,0:T(8,128)(2,1)S(1)}, bf16[128,128]{1,0:T(8,128)(2,1)S(1)}, u32[]{:S(2)}, u32[]{:S(2)}) collective-permute-start(bf16[128,128]{1,0:T(8,128)(2,1)S(1)} %copy-done.84), channel_id=1, source_target_pairs={{0,8},{8,16},{16,24},{24,28},{28,20},{20,12},{12,4},{4,0},{1,9},{9... | collective-permute-start | bytes 98312 | tf_op jit(solution)/shard_map/ppermute | solution.py:96
  117.0 14.0 %collective-permute-start.21 = (bf16[476,256]{1,0:T(8,128)(2,1)S(1)}, bf16[476,256]{1,0:T(8,128)(2,1)S(1)}, u32[]{:S(2)}, u32[]{:S(2)}) collective-permute-start(bf16[476,256]{1,0:T(8,128)(2,1)S(1)} %collective-permute-done.19), channel_id=1, source_target_pairs={{8,0},{16,8},{24,16},{28,24},{20,28},{12,20},{4,12},{0,4},{9,1},{1... | collective-permute-start | bytes 731144 | tf_op jit(solution)/shard_map/ppermute | solution.py:99
  148.4 150.2 %collective-permute-start.49 = (bf16[512,512]{1,0:T(8,128)(2,1)}, bf16[512,512]{1,0:T(8,128)(2,1)}, u32[]{:S(2)}, u32[]{:S(2)}) collective-permute-start(bf16[512,512]{1,0:T(8,128)(2,1)} %param.73), channel_id=1, source_target_pairs={{0,2},{1,3},{2,0},{3,1},{4,6},{5,7},{6,4},{7,5},{8,10},{9,11},{10,... | collective-permute-start | bytes 1572872 | tf_op jit(solution)/shard_map/ppermute | solution.py:32
  153.9 147.4 %collective-permute-start.52 = (bf16[512,512]{1,0:T(8,128)(2,1)}, bf16[512,512]{1,0:T(8,128)(2,1)}, u32[]{:S(2)}, u32[]{:S(2)}) collective-permute-start(bf16[512,512]{1,0:T(8,128)(2,1)} %param.74), channel_id=1, source_target_pairs={{0,2},{1,3},{2,0},{3,1},{4,6},{5,7},{6,4},{7,5},{8,10},{9,11},{10,... | collective-permute-start | bytes 1572872 | tf_op jit(solution)/shard_map/ppermute | solution.py:32
  154.5 96.7 %collective-permute-start.41 = (bf16[128,128]{1,0:T(8,128)(2,1)S(1)}, bf16[128,128]{1,0:T(8,128)(2,1)S(1)}, u32[]{:S(2)}, u32[]{:S(2)}) collective-permute-start(bf16[128,128]{1,0:T(8,128)(2,1)S(1)} %collective-permute-done.39), channel_id=1, source_target_pairs={{8,0},{16,8},{24,16},{28,24},{20,28},{12,20},{4,12},{0,4},{9,1},{1... | collective-permute-start | bytes 98312 | tf_op jit(solution)/shard_map/ppermute | solution.py:99
  246.6 56.1 %all-to-all-start = ((bf16[8,476,128]{2,1,0:T(8,128)(2,1)}), bf16[8,476,128]{2,1,0:T(8,128)(2,1)S(1)}, u32[]{:S(2)}, u32[]{:S(2)}) async-start(bf16[8,476,128]{2,1,0:T(8,128)(2,1)} %copy.105), calls=%async_computation | async-start | bytes 1966080 | tf_op jit(solution)/shard_map/all_to_all | solution.py:107
  251.1 473.0 %reduce-scatter.15.cloned.1.call-start = ((), (), s32[]{:S(2)}) async-start(), calls=%async_computation.14 | async-start | bytes 294912 | tf_op jit(solution)/shard_map/reduce_scatter | solution.py:112
  251.2 15.7 %collective-permute-start.42 = (bf16[128,128]{1,0:T(8,128)(2,1)S(1)}, bf16[128,128]{1,0:T(8,128)(2,1)S(1)}, u32[]{:S(2)}, u32[]{:S(2)}) collective-permute-start(bf16[128,128]{1,0:T(8,128)(2,1)S(1)} %collective-permute-done.40), channel_id=1, source_target_pairs={{0,8},{8,16},{16,24},{24,28},{28,20},{20,12},{12,4},{4,0},{1,9},{9... | collective-permute-start | bytes 98312 | tf_op jit(solution)/shard_map/ppermute | solution.py:96
  283.6 14.8 %collective-permute-start.59 = (bf16[816,128]{1,0:T(8,128)(2,1)S(1)}, bf16[816,128]{1,0:T(8,128)(2,1)S(1)}, u32[]{:S(2)}, u32[]{:S(2)}) collective-permute-start(bf16[816,128]{1,0:T(8,128)(2,1)S(1)} %copy-done.81), channel_id=1, source_target_pairs={{0,3},{1,2},{2,1},{3,0},{4,7},{5,6},{6,5},{7,4},{8,11},{9,10},{10,... | collective-permute-start | bytes 626696 | tf_op jit(solution)/shard_map/ppermute | solution.py:32
  402.4 17.8 %collective-permute-start.63 = (bf16[816,128]{1,0:T(8,128)(2,1)}, bf16[816,128]{1,0:T(8,128)(2,1)}, u32[]{:S(2)}, u32[]{:S(2)}) collective-permute-start(bf16[816,128]{1,0:T(8,128)(2,1)} %get-tuple-element.412), channel_id=1, source_target_pairs={{0,1},{1,0},{2,3},{3,2},{4,5},{5,4},{6,7},{7,6},{8,9},{9,8},{10,11... | collective-permute-start | bytes 626696 | tf_op jit(solution)/shard_map/ppermute | solution.py:32
  403.1 17.1 %collective-permute-start.64 = (bf16[816,128]{1,0:T(8,128)(2,1)}, bf16[816,128]{1,0:T(8,128)(2,1)}, u32[]{:S(2)}, u32[]{:S(2)}) collective-permute-start(bf16[816,128]{1,0:T(8,128)(2,1)} %get-tuple-element.329), channel_id=1, source_target_pairs={{0,2},{1,3},{2,0},{3,1},{4,6},{5,7},{6,4},{7,5},{8,10},{9,11},{10,... | collective-permute-start | bytes 626696 | tf_op jit(solution)/shard_map/ppermute | solution.py:32
  407.8 25.1 %collective-permute-start.86 = (bf16[512,512]{1,0:T(8,128)(2,1)}, bf16[512,512]{1,0:T(8,128)(2,1)}, u32[]{:S(2)}, u32[]{:S(2)}) collective-permute-start(bf16[512,512]{1,0:T(8,128)(2,1)} %get-tuple-element.342), channel_id=1, source_target_pairs={{0,1},{1,0},{2,3},{3,2},{4,5},{5,4},{6,7},{7,6},{8,9},{9,8},{10,11... | collective-permute-start | bytes 1572872 | tf_op jit(solution)/shard_map/ppermute | solution.py:32
  410.6 54.8 %collective-permute-start.85 = (bf16[512,512]{1,0:T(8,128)(2,1)}, bf16[512,512]{1,0:T(8,128)(2,1)}, u32[]{:S(2)}, u32[]{:S(2)}) collective-permute-start(bf16[512,512]{1,0:T(8,128)(2,1)} %get-tuple-element.341), channel_id=1, source_target_pairs={{0,1},{1,0},{2,3},{3,2},{4,5},{5,4},{6,7},{7,6},{8,9},{9,8},{10,11... | collective-permute-start | bytes 1572872 | tf_op jit(solution)/shard_map/ppermute | solution.py:32
  420.2 18.3 %collective-permute-start.89 = (bf16[512,512]{1,0:T(8,128)(2,1)}, bf16[512,512]{1,0:T(8,128)(2,1)}, u32[]{:S(2)}, u32[]{:S(2)}) collective-permute-start(bf16[512,512]{1,0:T(8,128)(2,1)} %get-tuple-element.344), channel_id=1, source_target_pairs={{0,1},{1,0},{2,3},{3,2},{4,5},{5,4},{6,7},{7,6},{8,9},{9,8},{10,11... | collective-permute-start | bytes 1572872 | tf_op jit(solution)/shard_map/ppermute | solution.py:32
  420.7 21.3 %collective-permute-start.82 = (bf16[1024,128]{1,0:T(8,128)(2,1)}, bf16[1024,128]{1,0:T(8,128)(2,1)}, u32[]{:S(2)}, u32[]{:S(2)}) collective-permute-start(bf16[1024,128]{1,0:T(8,128)(2,1)} %get-tuple-element.353), channel_id=1, source_target_pairs={{0,1},{1,0},{2,3},{3,2},{4,5},{5,4},{6,7},{7,6},{8,9},{9,8},{10,11... | collective-permute-start | bytes 786440 | tf_op jit(solution)/shard_map/ppermute | solution.py:32
  436.8 28.6 %collective-permute-start.87 = (bf16[512,512]{1,0:T(8,128)(2,1)}, bf16[512,512]{1,0:T(8,128)(2,1)}, u32[]{:S(2)}, u32[]{:S(2)}) collective-permute-start(bf16[512,512]{1,0:T(8,128)(2,1)} %add_convert_fusion.11), channel_id=1, source_target_pairs={{0,2},{1,3},{2,0},{3,1},{4,6},{5,7},{6,4},{7,5},{8,10},{9,11},{10,... | collective-permute-start | bytes 1572872 | tf_op jit(solution)/shard_map/ppermute | solution.py:32
  438.5 25.5 %collective-permute-start.67 = (f32[476,256]{1,0:T(8,128)}, f32[476,256]{1,0:T(8,128)}, u32[]{:S(2)}, u32[]{:S(2)}) collective-permute-start(f32[476,256]{1,0:T(8,128)} %maximum_add_fusion), channel_id=1, source_target_pairs={{0,2},{1,3},{2,0},{3,1},{4,6},{5,7},{6,4},{7,5},{8,10},{9,11},{10,... | collective-permute-start | bytes 1462280 | tf_op jit(solution)/shard_map/ppermute | solution.py:32
  442.0 26.6 %collective-permute-start.88 = (bf16[512,512]{1,0:T(8,128)(2,1)}, bf16[512,512]{1,0:T(8,128)(2,1)}, u32[]{:S(2)}, u32[]{:S(2)}) collective-permute-start(bf16[512,512]{1,0:T(8,128)(2,1)} %get-tuple-element.343), channel_id=1, source_target_pairs={{0,1},{1,0},{2,3},{3,2},{4,5},{5,4},{6,7},{7,6},{8,9},{9,8},{10,11... | collective-permute-start | bytes 1572872 | tf_op jit(solution)/shard_map/ppermute | solution.py:32
  442.2 32.1 %collective-permute-start.90 = (bf16[512,512]{1,0:T(8,128)(2,1)}, bf16[512,512]{1,0:T(8,128)(2,1)}, u32[]{:S(2)}, u32[]{:S(2)}) collective-permute-start(bf16[512,512]{1,0:T(8,128)(2,1)} %add_convert_fusion.9), channel_id=1, source_target_pairs={{0,2},{1,3},{2,0},{3,1},{4,6},{5,7},{6,4},{7,5},{8,10},{9,11},{10,... | collective-permute-start | bytes 1572872 | tf_op jit(solution)/shard_map/ppermute | solution.py:32
  445.4 385.2 %reduce-scatter.17.cloned.1.call-start = ((), (), s32[]{:S(2)}) async-start(), calls=%async_computation.15 | async-start | bytes 1179648 | tf_op jit(solution)/shard_map/reduce_scatter | solution.py:112
  477.1 405.3 %reduce-scatter.9.cloned.1.call-start = ((), (), s32[]{:S(2)}) async-start(), calls=%async_computation.11 | async-start | bytes 1769472 | tf_op jit(solution)/shard_map/reduce_scatter | solution.py:112
  486.8 26.1 %collective-permute-start.72 = (bf16[476,128]{1,0:T(8,128)(2,1)S(1)}, bf16[476,128]{1,0:T(8,128)(2,1)S(1)}, u32[]{:S(2)}, u32[]{:S(2)}) collective-permute-start(bf16[476,128]{1,0:T(8,128)(2,1)S(1)} %collective-permute-done.70), channel_id=1, source_target_pairs={{8,0},{16,8},{24,16},{28,24},{20,28},{12,20},{4,12},{0,4},{9,1},{1... | collective-permute-start | bytes 365576 | tf_op jit(solution)/shard_map/ppermute | solution.py:99
  490.8 23.4 %collective-permute-start.73 = (bf16[476,128]{1,0:T(8,128)(2,1)S(1)}, bf16[476,128]{1,0:T(8,128)(2,1)S(1)}, u32[]{:S(2)}, u32[]{:S(2)}) collective-permute-start(bf16[476,128]{1,0:T(8,128)(2,1)S(1)} %collective-permute-done.71), channel_id=1, source_target_pairs={{0,8},{8,16},{16,24},{24,28},{28,20},{20,12},{12,4},{4,0},{1,9},{9... | collective-permute-start | bytes 365576 | tf_op jit(solution)/shard_map/ppermute | solution.py:96
  512.9 38.2 %collective-permute-start.74 = (bf16[476,128]{1,0:T(8,128)(2,1)S(1)}, bf16[476,128]{1,0:T(8,128)(2,1)S(1)}, u32[]{:S(2)}, u32[]{:S(2)}) collective-permute-start(bf16[476,128]{1,0:T(8,128)(2,1)S(1)} %collective-permute-done.72), channel_id=1, source_target_pairs={{8,0},{16,8},{24,16},{28,24},{20,28},{12,20},{4,12},{0,4},{9,1},{1... | collective-permute-start | bytes 365576 | tf_op jit(solution)/shard_map/ppermute | solution.py:99
  514.2 49.9 %collective-permute-start.75 = (bf16[476,128]{1,0:T(8,128)(2,1)S(1)}, bf16[476,128]{1,0:T(8,128)(2,1)S(1)}, u32[]{:S(2)}, u32[]{:S(2)}) collective-permute-start(bf16[476,128]{1,0:T(8,128)(2,1)S(1)} %collective-permute-done.73), channel_id=1, source_target_pairs={{0,8},{8,16},{16,24},{24,28},{28,20},{20,12},{12,4},{4,0},{1,9},{9... | collective-permute-start | bytes 365576 | tf_op jit(solution)/shard_map/ppermute | solution.py:96
  517.6 380.4 %reduce-scatter.13.cloned.1.call-start = ((), (), s32[]{:S(2)}) async-start(), calls=%async_computation.13 | async-start | bytes 2359296 | tf_op jit(solution)/shard_map/reduce_scatter | solution.py:112
  704.3 14.4 %collective-permute-start.77 = (bf16[8,476,128]{2,0,1:T(8,128)(2,1)}, bf16[8,476,128]{2,0,1:T(8,128)(2,1)S(1)}, u32[]{:S(2)}, u32[]{:S(2)}) collective-permute-start(bf16[8,476,128]{2,0,1:T(8,128)(2,1)} %select_convert_fusion), channel_id=1, source_target_pairs={{0,1},{1,0},{2,3},{3,2},{4,5},{5,4},{6,7},{7,6},{8,9},{9,8},{10,11... | collective-permute-start | bytes 2924552 | tf_op jit(solution)/shard_map/ppermute | solution.py:32
  717.9 62.1 %collective-permute-start.76 = (bf16[8,476,128]{2,0,1:T(8,128)(2,1)}, bf16[8,476,128]{2,0,1:T(8,128)(2,1)}, u32[]{:S(2)}, u32[]{:S(2)}) collective-permute-start(bf16[8,476,128]{2,0,1:T(8,128)(2,1)} %get-tuple-element.319), channel_id=1, source_target_pairs={{0,1},{1,0},{2,3},{3,2},{4,5},{5,4},{6,7},{7,6},{8,9},{9,8},{10,11... | collective-permute-start | bytes 2924552 | tf_op jit(solution)/shard_map/ppermute | solution.py:32
  721.6 58.4 %collective-permute-start.78 = (bf16[8,476,128]{2,0,1:T(8,128)(2,1)}, bf16[8,476,128]{2,0,1:T(8,128)(2,1)S(1)}, u32[]{:S(2)}, u32[]{:S(2)}) collective-permute-start(bf16[8,476,128]{2,0,1:T(8,128)(2,1)} %add_convert_fusion.2), channel_id=1, source_target_pairs={{0,2},{1,3},{2,0},{3,1},{4,6},{5,7},{6,4},{7,5},{8,10},{9,11},{10,... | collective-permute-start | bytes 2924552 | tf_op jit(solution)/shard_map/ppermute | solution.py:32
  783.5 29.5 %all-to-all-start.1 = ((bf16[8,476,128]{2,1,0:T(8,128)(2,1)}), bf16[8,476,128]{2,1,0:T(8,128)(2,1)}, u32[]{:S(2)}, u32[]{:S(2)}) async-start(bf16[8,476,128]{2,1,0:T(8,128)(2,1)} %copy.120), calls=%async_computation.1 | async-start | bytes 1966080 | tf_op jit(solution)/shard_map/all_to_all | solution.py:107
  788.4 136.0 %reduce-scatter.7.cloned.1.call-start = ((), (), s32[]{:S(2)}) async-start(), calls=%async_computation.10 | async-start | bytes 1769472 | tf_op jit(solution)/shard_map/reduce_scatter | solution.py:112
  818.8 135.0 %reduce-scatter.11.cloned.1.call-start = ((), (), s32[]{:S(2)}) async-start(), calls=%async_computation.12 | async-start | bytes 2359296 | tf_op jit(solution)/shard_map/reduce_scatter | solution.py:112
  836.0 48.1 %collective-permute-start.93 = (bf16[128,512]{1,0:T(8,128)(2,1)}, bf16[128,512]{1,0:T(8,128)(2,1)S(1)}, u32[]{:S(2)}, u32[]{:S(2)}) collective-permute-start(bf16[128,512]{1,0:T(8,128)(2,1)} %collective-permute-done.91), channel_id=1, source_target_pairs={{0,8},{8,16},{16,24},{24,28},{28,20},{20,12},{12,4},{4,0},{1,9},{9... | collective-permute-start | bytes 393224 | tf_op jit(solution)/shard_map/ppermute | solution.py:96
  838.5 46.0 %collective-permute-start.94 = (bf16[128,512]{1,0:T(8,128)(2,1)}, bf16[128,512]{1,0:T(8,128)(2,1)S(1)}, u32[]{:S(2)}, u32[]{:S(2)}) collective-permute-start(bf16[128,512]{1,0:T(8,128)(2,1)} %collective-permute-done.92), channel_id=1, source_target_pairs={{8,0},{16,8},{24,16},{28,24},{20,28},{12,20},{4,12},{0,4},{9,1},{1... | collective-permute-start | bytes 393224 | tf_op jit(solution)/shard_map/ppermute | solution.py:99
  894.7 21.4 %collective-permute-start.81 = (bf16[3264,128]{1,0:T(8,128)(2,1)}, bf16[3264,128]{1,0:T(8,128)(2,1)}, u32[]{:S(2)}, u32[]{:S(2)}) collective-permute-start(bf16[3264,128]{1,0:T(8,128)(2,1)} %add_convert_fusion.3), channel_id=1, source_target_pairs={{0,2},{1,3},{2,0},{3,1},{4,6},{5,7},{6,4},{7,5},{8,10},{9,11},{10,... | collective-permute-start | bytes 2506760 | tf_op jit(solution)/shard_map/ppermute | solution.py:32
  (166 other events, 1555.0 us)
Sparse Core Ops, SparseCore 0:
  14.0 51.2 all-gather.2
  109.0 53.3 all-gather.4
  445.5 60.9 reduce-scatter.14
  510.3 62.6 reduce-scatter.16
  577.2 64.8 reduce-scatter.8
  710.8 69.0 reduce-scatter.12
  818.9 64.3 reduce-scatter.6
  887.2 66.5 reduce-scatter.10
where the time goes:
time: 975 us; the launch traced here: 963 us
  local copies, waits for them, and re-layouts  257 us (26%)
  waiting for transfers between devices  227 us (23%)
  other arithmetic  151 us (15%)
  matrix products  150 us (15%)
  starting transfers between devices  89.1 us (9%)
  blocking collectives  53.8 us (6%)
  between operations  35.3 us (4%)
    ppermute x56, waiting for transfers between devices, swap(): return lax.ppermute(value, 'tensor', [(i, i ^ mask) for i in range(4)])  81.5 us
    dot_general x9, matrix products, matmul(): return jnp.dot(left, right, preferred_element_type=F32)  65 us
    psum x1, blocking collectives, body(): sums = own_lanes(lax.psum(sums, ('dp', 'tensor')))  53.8 us
    ppermute x18, waiting for transfers between devices, ring_gather(): behind = lax.ppermute(behind, 'dp', down)  52.4 us
    dot_general x9, matrix products, against(): lax.dot_general(left, right, (((1,), (1,)), ((), ())), preferred_element_...  50.7 us
    ppermute x24, waiting for transfers between devices, ring_gather(): ahead = lax.ppermute(ahead, 'dp', up)  48.7 us
    scatter-add x15, other arithmetic, iso_backward(): total = total.at[j:j + span_len].add(spread[:, :, j * D:(j + 1) * D])  39.3 us
    unnamed x223, local copies, waits for them, and re-layouts  35.1 us
  transfers between devices with their start and end apart: 108, of which 41 were waited for; matrix products, arithmetic and copies ran while one was open for 50% of the time, Pallas kernels for 0%

commit v1 on v0

--- a/solution.py
+++ b/solution.py
@@ -340,7 +340,7 @@
             grad_last_bias,
         ]
     )
-    sums = own_lanes(lax.psum(sums, ("dp", "tensor")))
+    sums = own_lanes(lax.psum(lax.psum(sums, "dp"), "tensor"))
     return (
         series_out,
         grad_input,

time: 975 us -> 967 us (level)
    psum x1 -> x2, blocking collectives: 53.8 us -> 46.4 us  [body(): sums = own_lanes(lax.psum(lax.psum(sums, 'dp'), 'tensor'))]
  transfers between devices with their start and end apart: 108 -> 108, of which waited for: 41 -> 42; matrix products, arithmetic and copies ran while one was open for 50% -> 50% of each run, Pallas kernels for 0% -> 0%
where the time goes in v1:
time: 967 us; the launch traced here: 955 us
  local copies, waits for them, and re-layouts  257 us (27%)
  waiting for transfers between devices  226 us (23%)
  other arithmetic  151 us (16%)
  matrix products  150 us (16%)
  starting transfers between devices  89.2 us (9%)
  blocking collectives  46.4 us (5%)
  between operations  35.3 us (4%)
    ppermute x56, waiting for transfers between devices, swap(): return lax.ppermute(value, 'tensor', [(i, i ^ mask) for i in range(4)])  81.3 us
    dot_general x9, matrix products, matmul(): return jnp.dot(left, right, preferred_element_type=F32)  65.1 us
    ppermute x18, waiting for transfers between devices, ring_gather(): behind = lax.ppermute(behind, 'dp', down)  52.9 us
    dot_general x9, matrix products, against(): lax.dot_general(left, right, (((1,), (1,)), ((), ())), preferred_element_...  50.7 us
    ppermute x24, waiting for transfers between devices, ring_gather(): ahead = lax.ppermute(ahead, 'dp', up)  48.1 us
    psum x2, blocking collectives, body(): sums = own_lanes(lax.psum(lax.psum(sums, 'dp'), 'tensor'))  46.4 us
    scatter-add x15, other arithmetic, iso_backward(): total = total.at[j:j + span_len].add(spread[:, :, j * D:(j + 1) * D])  39.3 us
    unnamed x223, local copies, waits for them, and re-layouts  35.2 us
  transfers between devices with their start and end apart: 108, of which 42 were waited for; matrix products, arithmetic and copies ran while one was open for 50% of the time, Pallas kernels for 0%

profile of v1, /device:TPU:0, one launch (start us, length us, event | category | flops | bytes accessed | tf_op | source)
XLA Modules:
  0.0 954.9 jit_solution(3431091619947604045)
XLA Ops:
  41.1 11.8 %collective-permute-done.11 = bf16[1024,128]{1,0:T(8,128)(2,1)S(1)} collective-permute-done((bf16[1024,128]{1,0:T(8,128)(2,1)S(1)}, bf16[1024,128]{1,0:T(8,128)(2,1)S(1)}, u32[]{:S(2)}, u32[]{:S(2)}) %collective-permute-start.11) | collective-permute-done | bytes 262176 | tf_op jit(solution)/shard_map/ppermute | solution.py:99
  55.0 6.5 collective-permute-done.6
  80.7 4.2 collective-permute-done.16
  87.6 5.0 reshape.927
  101.8 4.3 collective-permute-done.17
  120.5 10.6 %collective-permute-done.21 = bf16[476,256]{1,0:T(8,128)(2,1)S(1)} collective-permute-done((bf16[476,256]{1,0:T(8,128)(2,1)S(1)}, bf16[476,256]{1,0:T(8,128)(2,1)S(1)}, u32[]{:S(2)}, u32[]{:S(2)}) %collective-permute-start.21) | collective-permute-done | bytes 243744 | tf_op jit(solution)/shard_map/ppermute | solution.py:99
  133.2 5.8 collective-permute-done.23
  172.7 21.0 %fusion.53 = bf16[8,4,68,128]{3,2,1,0:T(8,128)(2,1)S(1)} fusion(bf16[68,8,4,4608]{3,0,2,1:T(8,128)(2,1)S(1)} %bitcast.258, bf16[4608,128]{1,0:T(8,128)(2,1)} %constant_dynamic-update-slice_fusion), kind=kOutput, calls=%fused_computation.173 | convolution fusion | flops 2567192576 | bytes 21790720 | tf_op jit(solution)/shard_map/dot_general | solution.py:20
  212.5 22.6 %dot_general.101 = bf16[51,8,4,4096]{3,2,1,0:T(4,128)(2,1)} reshape(bf16[51,32,4096]{2,1,0:T(8,128)(2,1)} %fusion.38) | data formatting | bytes 26738688 | tf_op jit(solution)/shard_map/dot_general | solution.py:20
  235.1 10.3 %fusion.54 = bf16[8,4,51,128]{3,1,0,2:T(4,128)(2,1)S(1)} fusion(bf16[51,8,4,4096]{3,2,1,0:T(4,128)(2,1)} %dot_general.101, bf16[4096,128]{1,0:T(8,128)(2,1)} %constant_dynamic-update-slice_fusion.2), kind=kOutput, calls=%fused_computation.174 | convolution fusion | flops 1711484928 | bytes 14835712 | tf_op jit(solution)/shard_map/dot_general | solution.py:20
  246.7 4.5 all-to-all-start
  253.3 13.6 %collective-permute-done.42 = bf16[128,128]{1,0:T(8,128)(2,1)S(1)} collective-permute-done((bf16[128,128]{1,0:T(8,128)(2,1)S(1)}, bf16[128,128]{1,0:T(8,128)(2,1)S(1)}, u32[]{:S(2)}, u32[]{:S(2)}) %collective-permute-start.42) | collective-permute-done | bytes 32800 | tf_op jit(solution)/shard_map/ppermute | solution.py:96
  266.9 8.5 collective-permute-done.43
  284.2 4.9 collective-permute-done.58
  289.1 5.6 collective-permute-done.46
  350.4 19.6 %multiply_convert_fusion = (bf16[816,2048]{1,0:T(8,128)(2,1)S(1)}, f32[816,2048]{1,0:T(8,128)}, f32[816,2048]{1,0:T(8,128)}) fusion(bf16[512,512]{1,0:T(8,128)(2,1)S(1)} %copy-done.71, bf16[512,512]{1,0:T(8,128)(2,1)S(1)} %copy-done.70, bf16[512,512]{1,0:T(8,128)(2,1)S(1)} %copy-done.69, bf16[512,512]{1,0:T(8,128)(2,1)S(1)} %copy-done.68, ...), kind=kOutput, calls=%fused_computation.28 | convolution fusion | flops 1830379520 | bytes 20490624 | tf_op jit(solution)/shard_map/dot_general | solution.py:20
  373.7 7.2 add_convert_fusion
  445.7 18.4 %collective-permute-done.67 = f32[476,256]{1,0:T(8,128)} collective-permute-done((f32[476,256]{1,0:T(8,128)}, f32[476,256]{1,0:T(8,128)}, u32[]{:S(2)}, u32[]{:S(2)}) %collective-permute-start.67) | collective-permute-done | bytes 487456 | tf_op jit(solution)/shard_map/ppermute | solution.py:32
  468.9 5.5 collective-permute-done.90
  492.0 20.9 %copy.121 = bf16[68,32,4608]{2,1,0:T(8,128)(2,1)} copy(bf16[68,32,4608]{2,0,1:T(8,128)(2,1)} %copy-done.11) | data formatting | bytes 40108032 | tf_op jit(solution)/shard_map/concatenate | solution.py:150
  518.0 6.4 dynamic_update_slice.196
  524.9 6.4 dynamic_update_slice.197
  531.3 6.4 dynamic_update_slice.198
  538.1 6.4 dynamic_update_slice.199
  544.5 6.4 dynamic_update_slice.200
  551.3 6.4 dynamic_update_slice.201
  557.7 6.4 dynamic_update_slice.202
  564.3 6.4 dynamic_update_slice.203
  571.1 17.4 %fusion.56 = f32[68,32,4608]{2,1,0:T(8,128)} fusion(bf16[68,32,128]{2,1,0:T(8,128)(2,1)S(1)} %bitcast.272, bf16[4608,128]{1,0:T(8,128)(2,1)} %constant_dynamic-update-slice_fusion), kind=kOutput, calls=%fused_computation.176 | convolution fusion | flops 2566914048 | bytes 41844736 | tf_op jit(solution)/shard_map/dot_general | solution.py:28
  619.4 5.6 copy.116
  625.0 4.9 broadcast_in_dim.247
  629.8 22.2 %dynamic_update_slice.204 = f32[144,32,512]{2,0,1:T(8,128)} dynamic-update-slice(f32[144,32,512]{2,0,1:T(8,128)} %broadcast_in_dim.247, f32[76,32,512]{2,0,1:T(8,128)} %copy.116, s32[]{:T(128)S(6)} %select_n.1414, s32[]{:T(128)} %constant.1016.clone.1, s32[]{:T(128)} %constant.1016.clone.1) | dynamic-update-slice | bytes 9961476 | tf_op jit(solution)/shard_map/dynamic_update_slice | solution.py:171
  655.2 4.6 copy.117
  660.0 12.2 %fusion.61 = f32[51,32,4096]{2,1,0:T(8,128)} fusion(bf16[51,32,128]{2,1,0:T(8,128)(2,1)S(1)} %bitcast.274, bf16[4096,128]{1,0:T(8,128)(2,1)} %constant_dynamic-update-slice_fusion.2), kind=kOutput, calls=%fused_computation.185 | convolution fusion | flops 1711276032 | bytes 28205056 | tf_op jit(solution)/shard_map/dot_general | solution.py:28
  725.8 35.8 %psum.14 = f32[6,512]{1,0:T(8,128)S(1)} all-reduce(f32[6,512]{1,0:T(8,128)S(1)} %stack.49), channel_id=1, replica_groups=mesh['dp'=8,'tensor'=4] {'dp'}, use_global_device_ids=true, to_apply=%region_38.39 | all-reduce | flops 3072 | bytes 24576 | tf_op jit(solution)/shard_map/psum | solution.py:343
  761.6 10.6 %psum.15 = f32[6,512]{1,0:T(8,128)S(1)} all-reduce(f32[6,512]{1,0:T(8,128)S(1)} %psum.14), channel_id=1, replica_groups=mesh['dp'=8,'tensor'=4] {'tensor'}, use_global_device_ids=true, to_apply=%region_39.40 | all-reduce | flops 3072 | bytes 24576 | tf_op jit(solution)/shard_map/psum | solution.py:343
  776.2 4.2 all-to-all-start.1
  780.5 7.1 fusion.119
  788.9 15.4 %all-to-all-done.1 = bf16[8,476,128]{2,1,0:T(8,128)(2,1)} async-done(((bf16[8,476,128]{2,1,0:T(8,128)(2,1)}), bf16[8,476,128]{2,1,0:T(8,128)(2,1)}, u32[]{:S(2)}, u32[]{:S(2)}) %all-to-all-start.1) | async-done | bytes 974880 | tf_op jit(solution)/shard_map/all_to_all | solution.py:107
  810.2 10.2 %fusion.118 = f32[4608,128]{1,0:T(8,128)S(1)} fusion(bf16[2176,4608]{1,0:T(8,128)(2,1)} %bitcast.259, bf16[2176,128]{1,0:T(8,128)(2,1)} %bitcast.273), kind=kOutput, calls=%fused_computation.513 | convolution fusion | flops 2566914048 | bytes 22970368 | tf_op jit(solution)/shard_map/dot_general | solution.py:24
  835.9 8.4 reshape.948
  848.1 7.9 reshape.947
  856.0 9.4 add.1217
  868.1 4.3 select_convert_fusion.3
  882.2 4.2 add_convert_fusion.3
  891.9 15.9 %collective-permute-done.81 = bf16[3264,128]{1,0:T(8,128)(2,1)} collective-permute-done((bf16[3264,128]{1,0:T(8,128)(2,1)}, bf16[3264,128]{1,0:T(8,128)(2,1)}, u32[]{:S(2)}, u32[]{:S(2)}) %collective-permute-start.81) | collective-permute-done | bytes 835616 | tf_op jit(solution)/shard_map/ppermute | solution.py:32
  907.9 8.2 add_add_fusion
  917.8 28.0 %reduce-scatter.11.cloned.1.call-done = bf16[1024,128]{1,0:T(8,128)(2,1)} async-done(((bf16[8192,128]{1,0:T(8,128)(2,1)}), bf16[1024,128]{1,0:T(8,128)(2,1)}) %reduce-scatter.11.cloned.1.call-update) | async-done | bytes 262160 | tf_op jit(solution)/shard_map/reduce_scatter | solution.py:112
  (663 shorter events, 421.0 us)
Async XLA Ops:
  7.2 306.6 %all-gather.3.cloned.1.call-start = ((), (), s32[]{:S(2)}) async-start(), calls=%async_computation.8 | async-start | bytes 1769472 | tf_op jit(solution)/shard_map/all_gather | solution.py:210
  7.2 29.3 %collective-permute-start.3 = (bf16[768,128]{1,0:T(8,128)(2,1)}, bf16[768,128]{1,0:T(8,128)(2,1)}, u32[]{:S(2)}, u32[]{:S(2)}) collective-permute-start(bf16[768,128]{1,0:T(8,128)(2,1)} %param.66), channel_id=1, source_target_pairs={{0,8},{8,16},{16,24},{24,28},{28,20},{20,12},{12,4},{4,0},{1,9},{9... | collective-permute-start | bytes 589832 | tf_op jit(solution)/shard_map/ppermute | solution.py:96
  10.3 27.7 %collective-permute-start.4 = (bf16[768,128]{1,0:T(8,128)(2,1)}, bf16[768,128]{1,0:T(8,128)(2,1)}, u32[]{:S(2)}, u32[]{:S(2)}) collective-permute-start(bf16[768,128]{1,0:T(8,128)(2,1)} %param.66), channel_id=1, source_target_pairs={{8,0},{16,8},{24,16},{28,24},{20,28},{12,20},{4,12},{0,4},{9,1},{1... | collective-permute-start | bytes 589832 | tf_op jit(solution)/shard_map/ppermute | solution.py:99
  10.3 66.1 %collective-permute-start.1 = (bf16[3264,128]{1,0:T(8,128)(2,1)}, bf16[3264,128]{1,0:T(8,128)(2,1)S(1)}, u32[]{:S(2)}, u32[]{:S(2)}) collective-permute-start(bf16[3264,128]{1,0:T(8,128)(2,1)} %param.64), channel_id=1, source_target_pairs={{0,2},{1,3},{2,0},{3,1},{4,6},{5,7},{6,4},{7,5},{8,10},{9,11},{10,... | collective-permute-start | bytes 2506760 | tf_op jit(solution)/shard_map/ppermute | solution.py:32
  12.3 72.7 %collective-permute-start = (bf16[3264,128]{1,0:T(8,128)(2,1)}, bf16[3264,128]{1,0:T(8,128)(2,1)}, u32[]{:S(2)}, u32[]{:S(2)}) collective-permute-start(bf16[3264,128]{1,0:T(8,128)(2,1)} %param.64), channel_id=1, source_target_pairs={{0,1},{1,0},{2,3},{3,2},{4,5},{5,4},{6,7},{7,6},{8,9},{9,8},{10,11... | collective-permute-start | bytes 2506760 | tf_op jit(solution)/shard_map/ppermute | solution.py:32
  12.3 28.3 %collective-permute-start.10 = (bf16[1024,128]{1,0:T(8,128)(2,1)}, bf16[1024,128]{1,0:T(8,128)(2,1)S(1)}, u32[]{:S(2)}, u32[]{:S(2)}) collective-permute-start(bf16[1024,128]{1,0:T(8,128)(2,1)} %param.69), channel_id=1, source_target_pairs={{0,8},{8,16},{16,24},{24,28},{28,20},{20,12},{12,4},{4,0},{1,9},{9... | collective-permute-start | bytes 786440 | tf_op jit(solution)/shard_map/ppermute | solution.py:96
  13.9 305.4 %all-gather.5.cloned.1.call-start = ((), (), s32[]{:S(2)}) async-start(), calls=%async_computation.9 | async-start | bytes 2359296 | tf_op jit(solution)/shard_map/all_gather | solution.py:211
  36.5 16.4 %collective-permute-start.11 = (bf16[1024,128]{1,0:T(8,128)(2,1)S(1)}, bf16[1024,128]{1,0:T(8,128)(2,1)S(1)}, u32[]{:S(2)}, u32[]{:S(2)}) collective-permute-start(bf16[1024,128]{1,0:T(8,128)(2,1)S(1)} %copy-done.76), channel_id=1, source_target_pairs={{8,0},{16,8},{24,16},{28,24},{20,28},{12,20},{4,12},{0,4},{9,1},{1... | collective-permute-start | bytes 786440 | tf_op jit(solution)/shard_map/ppermute | solution.py:99
  38.0 15.2 %collective-permute-start.5 = (bf16[768,128]{1,0:T(8,128)(2,1)}, bf16[768,128]{1,0:T(8,128)(2,1)S(1)}, u32[]{:S(2)}, u32[]{:S(2)}) collective-permute-start(bf16[768,128]{1,0:T(8,128)(2,1)} %collective-permute-done.3), channel_id=1, source_target_pairs={{0,8},{8,16},{16,24},{24,28},{28,20},{20,12},{12,4},{4,0},{1,9},{9... | collective-permute-start | bytes 589832 | tf_op jit(solution)/shard_map/ppermute | solution.py:96
  40.6 20.9 %collective-permute-start.6 = (bf16[768,128]{1,0:T(8,128)(2,1)}, bf16[768,128]{1,0:T(8,128)(2,1)S(1)}, u32[]{:S(2)}, u32[]{:S(2)}) collective-permute-start(bf16[768,128]{1,0:T(8,128)(2,1)} %collective-permute-done.4), channel_id=1, source_target_pairs={{8,0},{16,8},{24,16},{28,24},{20,28},{12,20},{4,12},{0,4},{9,1},{1... | collective-permute-start | bytes 589832 | tf_op jit(solution)/shard_map/ppermute | solution.py:99
  53.2 14.9 %collective-permute-start.13 = (bf16[1024,128]{1,0:T(8,128)(2,1)S(1)}, bf16[1024,128]{1,0:T(8,128)(2,1)S(1)}, u32[]{:S(2)}, u32[]{:S(2)}) collective-permute-start(bf16[1024,128]{1,0:T(8,128)(2,1)S(1)} %collective-permute-done.11), channel_id=1, source_target_pairs={{8,0},{16,8},{24,16},{28,24},{20,28},{12,20},{4,12},{0,4},{9,1},{1... | collective-permute-start | bytes 786440 | tf_op jit(solution)/shard_map/ppermute | solution.py:99
  106.9 171.4 %collective-permute-start.30 = (f32[6,128]{1,0:T(8,128)S(1)}, f32[6,128]{1,0:T(8,128)S(1)}, u32[]{:S(2)}, u32[]{:S(2)}) collective-permute-start(f32[6,128]{1,0:T(8,128)S(1)} %stack.44), channel_id=1, source_target_pairs={{0,2},{1,3},{2,0},{3,1},{4,6},{5,7},{6,4},{7,5},{8,10},{9,11},{10,... | collective-permute-start | bytes 9224 | tf_op jit(solution)/shard_map/ppermute | solution.py:32
  107.5 173.6 %collective-permute-start.29 = (f32[6,128]{1,0:T(8,128)S(1)}, f32[6,128]{1,0:T(8,128)S(1)}, u32[]{:S(2)}, u32[]{:S(2)}) collective-permute-start(f32[6,128]{1,0:T(8,128)S(1)} %stack.44), channel_id=1, source_target_pairs={{0,1},{1,0},{2,3},{3,2},{4,5},{5,4},{6,7},{7,6},{8,9},{9,8},{10,11... | collective-permute-start | bytes 9224 | tf_op jit(solution)/shard_map/ppermute | solution.py:32
  107.5 41.1 %collective-permute-start.38 = (bf16[128,128]{1,0:T(8,128)(2,1)S(1)}, bf16[128,128]{1,0:T(8,128)(2,1)S(1)}, u32[]{:S(2)}, u32[]{:S(2)}) collective-permute-start(bf16[128,128]{1,0:T(8,128)(2,1)S(1)} %copy-done.84), channel_id=1, source_target_pairs={{0,8},{8,16},{16,24},{24,28},{28,20},{20,12},{12,4},{4,0},{1,9},{9... | collective-permute-start | bytes 98312 | tf_op jit(solution)/shard_map/ppermute | solution.py:96
  117.0 14.0 %collective-permute-start.21 = (bf16[476,256]{1,0:T(8,128)(2,1)S(1)}, bf16[476,256]{1,0:T(8,128)(2,1)S(1)}, u32[]{:S(2)}, u32[]{:S(2)}) collective-permute-start(bf16[476,256]{1,0:T(8,128)(2,1)S(1)} %collective-permute-done.19), channel_id=1, source_target_pairs={{8,0},{16,8},{24,16},{28,24},{20,28},{12,20},{4,12},{0,4},{9,1},{1... | collective-permute-start | bytes 731144 | tf_op jit(solution)/shard_map/ppermute | solution.py:99
  148.6 150.0 %collective-permute-start.49 = (bf16[512,512]{1,0:T(8,128)(2,1)}, bf16[512,512]{1,0:T(8,128)(2,1)}, u32[]{:S(2)}, u32[]{:S(2)}) collective-permute-start(bf16[512,512]{1,0:T(8,128)(2,1)} %param.73), channel_id=1, source_target_pairs={{0,2},{1,3},{2,0},{3,1},{4,6},{5,7},{6,4},{7,5},{8,10},{9,11},{10,... | collective-permute-start | bytes 1572872 | tf_op jit(solution)/shard_map/ppermute | solution.py:32
  154.0 147.4 %collective-permute-start.52 = (bf16[512,512]{1,0:T(8,128)(2,1)}, bf16[512,512]{1,0:T(8,128)(2,1)}, u32[]{:S(2)}, u32[]{:S(2)}) collective-permute-start(bf16[512,512]{1,0:T(8,128)(2,1)} %param.74), channel_id=1, source_target_pairs={{0,2},{1,3},{2,0},{3,1},{4,6},{5,7},{6,4},{7,5},{8,10},{9,11},{10,... | collective-permute-start | bytes 1572872 | tf_op jit(solution)/shard_map/ppermute | solution.py:32
  154.7 96.5 %collective-permute-start.41 = (bf16[128,128]{1,0:T(8,128)(2,1)S(1)}, bf16[128,128]{1,0:T(8,128)(2,1)S(1)}, u32[]{:S(2)}, u32[]{:S(2)}) collective-permute-start(bf16[128,128]{1,0:T(8,128)(2,1)S(1)} %collective-permute-done.39), channel_id=1, source_target_pairs={{8,0},{16,8},{24,16},{28,24},{20,28},{12,20},{4,12},{0,4},{9,1},{1... | collective-permute-start | bytes 98312 | tf_op jit(solution)/shard_map/ppermute | solution.py:99
  246.7 56.0 %all-to-all-start = ((bf16[8,476,128]{2,1,0:T(8,128)(2,1)}), bf16[8,476,128]{2,1,0:T(8,128)(2,1)S(1)}, u32[]{:S(2)}, u32[]{:S(2)}) async-start(bf16[8,476,128]{2,1,0:T(8,128)(2,1)} %copy.105), calls=%async_computation | async-start | bytes 1966080 | tf_op jit(solution)/shard_map/all_to_all | solution.py:107
  251.2 473.1 %reduce-scatter.15.cloned.1.call-start = ((), (), s32[]{:S(2)}) async-start(), calls=%async_computation.14 | async-start | bytes 294912 | tf_op jit(solution)/shard_map/reduce_scatter | solution.py:112
  251.2 15.7 %collective-permute-start.42 = (bf16[128,128]{1,0:T(8,128)(2,1)S(1)}, bf16[128,128]{1,0:T(8,128)(2,1)S(1)}, u32[]{:S(2)}, u32[]{:S(2)}) collective-permute-start(bf16[128,128]{1,0:T(8,128)(2,1)S(1)} %collective-permute-done.40), channel_id=1, source_target_pairs={{0,8},{8,16},{16,24},{24,28},{28,20},{20,12},{12,4},{4,0},{1,9},{9... | collective-permute-start | bytes 98312 | tf_op jit(solution)/shard_map/ppermute | solution.py:96
  283.6 14.8 %collective-permute-start.59 = (bf16[816,128]{1,0:T(8,128)(2,1)S(1)}, bf16[816,128]{1,0:T(8,128)(2,1)S(1)}, u32[]{:S(2)}, u32[]{:S(2)}) collective-permute-start(bf16[816,128]{1,0:T(8,128)(2,1)S(1)} %copy-done.81), channel_id=1, source_target_pairs={{0,3},{1,2},{2,1},{3,0},{4,7},{5,6},{6,5},{7,4},{8,11},{9,10},{10,... | collective-permute-start | bytes 626696 | tf_op jit(solution)/shard_map/ppermute | solution.py:32
  402.5 17.9 %collective-permute-start.63 = (bf16[816,128]{1,0:T(8,128)(2,1)}, bf16[816,128]{1,0:T(8,128)(2,1)}, u32[]{:S(2)}, u32[]{:S(2)}) collective-permute-start(bf16[816,128]{1,0:T(8,128)(2,1)} %get-tuple-element.412), channel_id=1, source_target_pairs={{0,1},{1,0},{2,3},{3,2},{4,5},{5,4},{6,7},{7,6},{8,9},{9,8},{10,11... | collective-permute-start | bytes 626696 | tf_op jit(solution)/shard_map/ppermute | solution.py:32
  403.2 17.2 %collective-permute-start.64 = (bf16[816,128]{1,0:T(8,128)(2,1)}, bf16[816,128]{1,0:T(8,128)(2,1)}, u32[]{:S(2)}, u32[]{:S(2)}) collective-permute-start(bf16[816,128]{1,0:T(8,128)(2,1)} %get-tuple-element.329), channel_id=1, source_target_pairs={{0,2},{1,3},{2,0},{3,1},{4,6},{5,7},{6,4},{7,5},{8,10},{9,11},{10,... | collective-permute-start | bytes 626696 | tf_op jit(solution)/shard_map/ppermute | solution.py:32
  407.8 25.2 %collective-permute-start.86 = (bf16[512,512]{1,0:T(8,128)(2,1)}, bf16[512,512]{1,0:T(8,128)(2,1)}, u32[]{:S(2)}, u32[]{:S(2)}) collective-permute-start(bf16[512,512]{1,0:T(8,128)(2,1)} %get-tuple-element.342), channel_id=1, source_target_pairs={{0,1},{1,0},{2,3},{3,2},{4,5},{5,4},{6,7},{7,6},{8,9},{9,8},{10,11... | collective-permute-start | bytes 1572872 | tf_op jit(solution)/shard_map/ppermute | solution.py:32
  410.7 54.8 %collective-permute-start.85 = (bf16[512,512]{1,0:T(8,128)(2,1)}, bf16[512,512]{1,0:T(8,128)(2,1)}, u32[]{:S(2)}, u32[]{:S(2)}) collective-permute-start(bf16[512,512]{1,0:T(8,128)(2,1)} %get-tuple-element.341), channel_id=1, source_target_pairs={{0,1},{1,0},{2,3},{3,2},{4,5},{5,4},{6,7},{7,6},{8,9},{9,8},{10,11... | collective-permute-start | bytes 1572872 | tf_op jit(solution)/shard_map/ppermute | solution.py:32
  420.4 18.3 %collective-permute-start.89 = (bf16[512,512]{1,0:T(8,128)(2,1)}, bf16[512,512]{1,0:T(8,128)(2,1)}, u32[]{:S(2)}, u32[]{:S(2)}) collective-permute-start(bf16[512,512]{1,0:T(8,128)(2,1)} %get-tuple-element.344), channel_id=1, source_target_pairs={{0,1},{1,0},{2,3},{3,2},{4,5},{5,4},{6,7},{7,6},{8,9},{9,8},{10,11... | collective-permute-start | bytes 1572872 | tf_op jit(solution)/shard_map/ppermute | solution.py:32
  420.9 21.3 %collective-permute-start.82 = (bf16[1024,128]{1,0:T(8,128)(2,1)}, bf16[1024,128]{1,0:T(8,128)(2,1)}, u32[]{:S(2)}, u32[]{:S(2)}) collective-permute-start(bf16[1024,128]{1,0:T(8,128)(2,1)} %get-tuple-element.353), channel_id=1, source_target_pairs={{0,1},{1,0},{2,3},{3,2},{4,5},{5,4},{6,7},{7,6},{8,9},{9,8},{10,11... | collective-permute-start | bytes 786440 | tf_op jit(solution)/shard_map/ppermute | solution.py:32
  436.9 28.6 %collective-permute-start.87 = (bf16[512,512]{1,0:T(8,128)(2,1)}, bf16[512,512]{1,0:T(8,128)(2,1)}, u32[]{:S(2)}, u32[]{:S(2)}) collective-permute-start(bf16[512,512]{1,0:T(8,128)(2,1)} %add_convert_fusion.11), channel_id=1, source_target_pairs={{0,2},{1,3},{2,0},{3,1},{4,6},{5,7},{6,4},{7,5},{8,10},{9,11},{10,... | collective-permute-start | bytes 1572872 | tf_op jit(solution)/shard_map/ppermute | solution.py:32
  438.7 25.5 %collective-permute-start.67 = (f32[476,256]{1,0:T(8,128)}, f32[476,256]{1,0:T(8,128)}, u32[]{:S(2)}, u32[]{:S(2)}) collective-permute-start(f32[476,256]{1,0:T(8,128)} %maximum_add_fusion), channel_id=1, source_target_pairs={{0,2},{1,3},{2,0},{3,1},{4,6},{5,7},{6,4},{7,5},{8,10},{9,11},{10,... | collective-permute-start | bytes 1462280 | tf_op jit(solution)/shard_map/ppermute | solution.py:32
  442.2 26.6 %collective-permute-start.88 = (bf16[512,512]{1,0:T(8,128)(2,1)}, bf16[512,512]{1,0:T(8,128)(2,1)}, u32[]{:S(2)}, u32[]{:S(2)}) collective-permute-start(bf16[512,512]{1,0:T(8,128)(2,1)} %get-tuple-element.343), channel_id=1, source_target_pairs={{0,1},{1,0},{2,3},{3,2},{4,5},{5,4},{6,7},{7,6},{8,9},{9,8},{10,11... | collective-permute-start | bytes 1572872 | tf_op jit(solution)/shard_map/ppermute | solution.py:32
  442.3 32.1 %collective-permute-start.90 = (bf16[512,512]{1,0:T(8,128)(2,1)}, bf16[512,512]{1,0:T(8,128)(2,1)}, u32[]{:S(2)}, u32[]{:S(2)}) collective-permute-start(bf16[512,512]{1,0:T(8,128)(2,1)} %add_convert_fusion.9), channel_id=1, source_target_pairs={{0,2},{1,3},{2,0},{3,1},{4,6},{5,7},{6,4},{7,5},{8,10},{9,11},{10,... | collective-permute-start | bytes 1572872 | tf_op jit(solution)/shard_map/ppermute | solution.py:32
  445.5 376.5 %reduce-scatter.17.cloned.1.call-start = ((), (), s32[]{:S(2)}) async-start(), calls=%async_computation.15 | async-start | bytes 1179648 | tf_op jit(solution)/shard_map/reduce_scatter | solution.py:112
  477.3 397.0 %reduce-scatter.9.cloned.1.call-start = ((), (), s32[]{:S(2)}) async-start(), calls=%async_computation.11 | async-start | bytes 1769472 | tf_op jit(solution)/shard_map/reduce_scatter | solution.py:112
  486.9 26.0 %collective-permute-start.72 = (bf16[476,128]{1,0:T(8,128)(2,1)S(1)}, bf16[476,128]{1,0:T(8,128)(2,1)S(1)}, u32[]{:S(2)}, u32[]{:S(2)}) collective-permute-start(bf16[476,128]{1,0:T(8,128)(2,1)S(1)} %collective-permute-done.70), channel_id=1, source_target_pairs={{8,0},{16,8},{24,16},{28,24},{20,28},{12,20},{4,12},{0,4},{9,1},{1... | collective-permute-start | bytes 365576 | tf_op jit(solution)/shard_map/ppermute | solution.py:99
  491.0 23.3 %collective-permute-start.73 = (bf16[476,128]{1,0:T(8,128)(2,1)S(1)}, bf16[476,128]{1,0:T(8,128)(2,1)S(1)}, u32[]{:S(2)}, u32[]{:S(2)}) collective-permute-start(bf16[476,128]{1,0:T(8,128)(2,1)S(1)} %collective-permute-done.71), channel_id=1, source_target_pairs={{0,8},{8,16},{16,24},{24,28},{28,20},{20,12},{12,4},{4,0},{1,9},{9... | collective-permute-start | bytes 365576 | tf_op jit(solution)/shard_map/ppermute | solution.py:96
  512.9 38.2 %collective-permute-start.74 = (bf16[476,128]{1,0:T(8,128)(2,1)S(1)}, bf16[476,128]{1,0:T(8,128)(2,1)S(1)}, u32[]{:S(2)}, u32[]{:S(2)}) collective-permute-start(bf16[476,128]{1,0:T(8,128)(2,1)S(1)} %collective-permute-done.72), channel_id=1, source_target_pairs={{8,0},{16,8},{24,16},{28,24},{20,28},{12,20},{4,12},{0,4},{9,1},{1... | collective-permute-start | bytes 365576 | tf_op jit(solution)/shard_map/ppermute | solution.py:99
  514.2 49.9 %collective-permute-start.75 = (bf16[476,128]{1,0:T(8,128)(2,1)S(1)}, bf16[476,128]{1,0:T(8,128)(2,1)S(1)}, u32[]{:S(2)}, u32[]{:S(2)}) collective-permute-start(bf16[476,128]{1,0:T(8,128)(2,1)S(1)} %collective-permute-done.73), channel_id=1, source_target_pairs={{0,8},{8,16},{16,24},{24,28},{28,20},{20,12},{12,4},{4,0},{1,9},{9... | collective-permute-start | bytes 365576 | tf_op jit(solution)/shard_map/ppermute | solution.py:96
  517.7 372.3 %reduce-scatter.13.cloned.1.call-start = ((), (), s32[]{:S(2)}) async-start(), calls=%async_computation.13 | async-start | bytes 2359296 | tf_op jit(solution)/shard_map/reduce_scatter | solution.py:112
  704.4 14.4 %collective-permute-start.77 = (bf16[8,476,128]{2,0,1:T(8,128)(2,1)}, bf16[8,476,128]{2,0,1:T(8,128)(2,1)S(1)}, u32[]{:S(2)}, u32[]{:S(2)}) collective-permute-start(bf16[8,476,128]{2,0,1:T(8,128)(2,1)} %select_convert_fusion), channel_id=1, source_target_pairs={{0,1},{1,0},{2,3},{3,2},{4,5},{5,4},{6,7},{7,6},{8,9},{9,8},{10,11... | collective-permute-start | bytes 2924552 | tf_op jit(solution)/shard_map/ppermute | solution.py:32
  718.1 54.7 %collective-permute-start.76 = (bf16[8,476,128]{2,0,1:T(8,128)(2,1)}, bf16[8,476,128]{2,0,1:T(8,128)(2,1)}, u32[]{:S(2)}, u32[]{:S(2)}) collective-permute-start(bf16[8,476,128]{2,0,1:T(8,128)(2,1)} %get-tuple-element.319), channel_id=1, source_target_pairs={{0,1},{1,0},{2,3},{3,2},{4,5},{5,4},{6,7},{7,6},{8,9},{9,8},{10,11... | collective-permute-start | bytes 2924552 | tf_op jit(solution)/shard_map/ppermute | solution.py:32
  721.6 51.1 %collective-permute-start.78 = (bf16[8,476,128]{2,0,1:T(8,128)(2,1)}, bf16[8,476,128]{2,0,1:T(8,128)(2,1)S(1)}, u32[]{:S(2)}, u32[]{:S(2)}) collective-permute-start(bf16[8,476,128]{2,0,1:T(8,128)(2,1)} %add_convert_fusion.2), channel_id=1, source_target_pairs={{0,2},{1,3},{2,0},{3,1},{4,6},{5,7},{6,4},{7,5},{8,10},{9,11},{10,... | collective-permute-start | bytes 2924552 | tf_op jit(solution)/shard_map/ppermute | solution.py:32
  776.2 28.1 %all-to-all-start.1 = ((bf16[8,476,128]{2,1,0:T(8,128)(2,1)}), bf16[8,476,128]{2,1,0:T(8,128)(2,1)}, u32[]{:S(2)}, u32[]{:S(2)}) async-start(bf16[8,476,128]{2,1,0:T(8,128)(2,1)} %copy.120), calls=%async_computation.1 | async-start | bytes 1966080 | tf_op jit(solution)/shard_map/all_to_all | solution.py:107
  780.5 135.6 %reduce-scatter.7.cloned.1.call-start = ((), (), s32[]{:S(2)}) async-start(), calls=%async_computation.10 | async-start | bytes 1769472 | tf_op jit(solution)/shard_map/reduce_scatter | solution.py:112
  810.2 135.6 %reduce-scatter.11.cloned.1.call-start = ((), (), s32[]{:S(2)}) async-start(), calls=%async_computation.12 | async-start | bytes 2359296 | tf_op jit(solution)/shard_map/reduce_scatter | solution.py:112
  827.3 48.7 %collective-permute-start.93 = (bf16[128,512]{1,0:T(8,128)(2,1)}, bf16[128,512]{1,0:T(8,128)(2,1)S(1)}, u32[]{:S(2)}, u32[]{:S(2)}) collective-permute-start(bf16[128,512]{1,0:T(8,128)(2,1)} %collective-permute-done.91), channel_id=1, source_target_pairs={{0,8},{8,16},{16,24},{24,28},{28,20},{20,12},{12,4},{4,0},{1,9},{9... | collective-permute-start | bytes 393224 | tf_op jit(solution)/shard_map/ppermute | solution.py:96
  829.7 46.3 %collective-permute-start.94 = (bf16[128,512]{1,0:T(8,128)(2,1)}, bf16[128,512]{1,0:T(8,128)(2,1)S(1)}, u32[]{:S(2)}, u32[]{:S(2)}) collective-permute-start(bf16[128,512]{1,0:T(8,128)(2,1)} %collective-permute-done.92), channel_id=1, source_target_pairs={{8,0},{16,8},{24,16},{28,24},{20,28},{12,20},{4,12},{0,4},{9,1},{1... | collective-permute-start | bytes 393224 | tf_op jit(solution)/shard_map/ppermute | solution.py:99
  886.4 21.4 %collective-permute-start.81 = (bf16[3264,128]{1,0:T(8,128)(2,1)}, bf16[3264,128]{1,0:T(8,128)(2,1)}, u32[]{:S(2)}, u32[]{:S(2)}) collective-permute-start(bf16[3264,128]{1,0:T(8,128)(2,1)} %add_convert_fusion.3), channel_id=1, source_target_pairs={{0,2},{1,3},{2,0},{3,1},{4,6},{5,7},{6,4},{7,5},{8,10},{9,11},{10,... | collective-permute-start | bytes 2506760 | tf_op jit(solution)/shard_map/ppermute | solution.py:32
  (166 other events, 1552.6 us)
Sparse Core Ops, SparseCore 0:
  14.0 51.2 all-gather.2
  109.0 53.3 all-gather.4
  445.6 60.8 reduce-scatter.14
  510.4 62.5 reduce-scatter.16
  577.3 64.7 reduce-scatter.8
  711.0 68.7 reduce-scatter.12
  810.3 65.0 reduce-scatter.6
  879.4 66.3 reduce-scatter.10
